TPU v7x, 512 devices: a whole 4x8x8 slice. The times are simulated.
512 devices in a mesh: wide: 64 (over z, y), field: 8 (over x, core).
Axes of the slice: x: 4, y: 8, z: 8, core: 2. Of those that a mesh axis runs over, the one named last changes fastest.
Arguments:
- fine_field_in: bfloat16 [2048, 128, 512], P('wide', 'field'), may hold values from -6 to 6
- fine_points: float32 [4096, 3, 1024], P(('wide', 'field')), may hold values from -1 to 1
- coarse_points: float32 [4096, 3, 1024], P(('wide', 'field')), may hold values from -1 to 1
- quad_weights: float32 [4096, 1024], P(('wide', 'field')), may hold values from 0.00390625 to 0.01171875
- pair_fine: int32 [4096], P('wide'), may hold values from 0 to 31, as said below
- pair_owner: int32 [4096, 1], P('wide'), may hold values from 0 to 63; in each aligned block of 64 rows (0 to 63, 64 to 127, ...) at most 2 rows name the same one
- pair_coarse: int32 [4096], P('wide'), may hold values from 0 to 15
- coarse_faces: int32 [1024, 6], P('wide'), may hold values from 0 to 1023, as said below
- coarse_inv_mass: float32 [1024], P('wide'), may hold values from 0.5 to 2
- fine_inv_mass: float32 [2048], P('wide'), may hold values from 0.5 to 2
Outputs:
- coarse_field: bfloat16 [1024, 128, 512], P('wide', 'field')
- fine_field: bfloat16 [2048, 128, 512], P('wide', 'field')
Inputs may be any that keep to these rules, and one draw needn't show every extreme that they name: `pair_fine`: within each aligned block of 64 pairs (one partition) every value 0 to 31 appears at least once. `pair_owner`: in each aligned block of 64 rows (one partition) no owner is named more than 2 times, a bound that some block reaches. `coarse_faces`: the owner of a neighbour (index // 16) differs from the element's own owner by at most one; a boundary face names the element itself.
All inputs are finite; a program needn't handle non-finite values.
Results may differ from a plain program's by a relative error of at most 0.007.
Values may be sent and summed in bfloat16 or wider, within the bound.
A program may use at most 64 MiB of HBM per device.

v0:
```python
import math

import jax
import jax.numpy as jnp
from jax import lax
from jax.sharding import PartitionSpec as P

NB = 8
CAP = 2


DIFFUSE = 0.125


def with_halo(block, sides, width):
    for axis, dim in sides:
        count = lax.axis_size(axis)
        forward = [(i, i + 1) for i in range(count - 1)]
        backward = [(target, source) for source, target in forward]
        low = lax.ppermute(
            lax.slice_in_dim(block, block.shape[dim] - width, None, axis=dim), axis, forward
        )
        high = lax.ppermute(lax.slice_in_dim(block, 0, width, axis=dim), axis, backward)
        block = jnp.concatenate([low, block, high], axis=dim)
    return block


def legendre(points, count):
    values = [jnp.ones_like(points), points]
    for degree in range(1, count - 1):
        values.append(
            ((2 * degree + 1) * points * values[degree] - degree * values[degree - 1])
            / (degree + 1)
        )
    values = values[:count]
    return jnp.stack([values[n] * math.sqrt((2 * n + 1) / 2.0) for n in range(count)])


def basis(points, count):
    table = legendre(points, count)
    product = table[:, None, None, 0, :] * table[None, :, None, 1, :] * table[None, None, :, 2, :]
    return product.reshape(count * count * count, points.shape[-1])


def build_tile(fine_pts, coarse_pts, weights):
    left = (basis(coarse_pts, NB) * weights[None, :]).astype(jnp.bfloat16)
    right = basis(fine_pts, NB).astype(jnp.bfloat16)
    return lax.dot_general(
        left, right, (((1,), (1,)), ((), ())), preferred_element_type=jnp.float32
    ).astype(jnp.bfloat16)


def shards(
    fine_field_in,
    fine_points,
    coarse_points,
    quad_weights,
    pair_fine,
    pair_owner,
    pair_coarse,
    coarse_faces,
    coarse_inv_mass,
    fine_inv_mass,
):
    nwide = lax.axis_size("wide")
    wide_index = lax.axis_index("wide")
    grp_pairs = pair_fine.shape[0]
    block = fine_field_in.shape[1]
    basis_count = fine_field_in.shape[2]
    fine_count = fine_field_in.shape[0]
    coarse_count = coarse_inv_mass.shape[0]
    slots = nwide * CAP
    tiles = lax.map(
        lambda item: build_tile(item[0], item[1], item[2]),
        (fine_points, coarse_points, quad_weights),
    )
    picked = jnp.take(fine_field_in, pair_fine, axis=0)
    rows = lax.all_to_all(picked, "field", split_axis=0, concat_axis=1, tiled=True)
    contrib = jnp.einsum("pfj,pij->pfi", rows, tiles, preferred_element_type=jnp.float32).astype(
        jnp.bfloat16
    )
    blocked = lax.all_to_all(contrib, "field", split_axis=1, concat_axis=0, tiled=True)
    owner = pair_owner[:, 0]
    owner_hot = (owner[:, None] == jnp.arange(nwide, dtype=jnp.int32)[None, :]).astype(jnp.int32)
    before = jnp.cumsum(owner_hot, axis=0) - owner_hot
    slot = jnp.sum(before * owner_hot, axis=1)
    target = owner * CAP + slot
    place = jnp.arange(slots, dtype=jnp.int32)[:, None] == target[None, :]
    place_bf = place.astype(jnp.bfloat16)
    slot_ids = jnp.sum(jnp.where(place, (pair_coarse + 1)[None, :], 0), axis=1)
    outgoing = jnp.dot(
        place_bf,
        blocked.reshape(grp_pairs, block * basis_count),
        preferred_element_type=jnp.float32,
    ).astype(jnp.bfloat16)
    arrived, arrived_ids = (
        lax.all_to_all(outgoing, "wide", split_axis=0, concat_axis=0, tiled=True),
        lax.all_to_all(slot_ids, "wide", split_axis=0, concat_axis=0, tiled=True),
    )
    owned_hot = (
        jnp.arange(coarse_count, dtype=jnp.int32)[:, None] == (arrived_ids - 1)[None, :]
    ).astype(jnp.bfloat16)
    load = jnp.dot(owned_hot, arrived, preferred_element_type=jnp.float32)
    solved = coarse_inv_mass[:, None] * load
    table = with_halo(solved, (("wide", 0),), coarse_count)
    relative = coarse_faces - (wide_index - 1) * coarse_count
    face_hits = jnp.sum(
        (
            relative[:, :, None] == jnp.arange(3 * coarse_count, dtype=jnp.int32)[None, None, :]
        ).astype(jnp.float32),
        axis=1,
    )
    beside = jnp.dot(
        face_hits, table, precision=lax.Precision.HIGHEST, preferred_element_type=jnp.float32
    )
    smoothed = solved + DIFFUSE * (beside - 6.0 * solved)
    coarse_out = smoothed.astype(jnp.bfloat16)
    reply = lax.dot_general(
        owned_hot, coarse_out, (((0,), (0,)), ((), ())), preferred_element_type=jnp.float32
    ).astype(jnp.bfloat16)
    returned = lax.all_to_all(reply, "wide", split_axis=0, concat_axis=0, tiled=True)
    per_pair = lax.dot_general(
        place_bf, returned, (((0,), (0,)), ((), ())), preferred_element_type=jnp.float32
    ).astype(jnp.bfloat16)
    spread = lax.all_to_all(
        per_pair.reshape(grp_pairs, block, basis_count),
        "field",
        split_axis=0,
        concat_axis=1,
        tiled=True,
    )
    terms = jnp.einsum("pfj,pji->pfi", spread, tiles, preferred_element_type=jnp.float32).astype(
        jnp.bfloat16
    )
    collected = lax.all_to_all(terms, "field", split_axis=1, concat_axis=0, tiled=True)
    fine_hot = (jnp.arange(fine_count, dtype=jnp.int32)[:, None] == pair_fine[None, :]).astype(
        jnp.bfloat16
    )
    fine_sum = jnp.dot(
        fine_hot,
        collected.reshape(grp_pairs, block * basis_count),
        preferred_element_type=jnp.float32,
    )
    fine_out = (fine_inv_mass[:, None] * fine_sum).astype(jnp.bfloat16)
    return (
        coarse_out.reshape(coarse_count, block, basis_count),
        fine_out.reshape(fine_count, block, basis_count),
    )


def solution(mesh):
    placed = (
        P("wide", "field", None),
        P(("wide", "field"), None, None),
        P(("wide", "field"), None, None),
        P(("wide", "field"), None),
        P("wide"),
        P("wide", None),
        P("wide"),
        P("wide", None),
        P("wide"),
        P("wide"),
    )
    return jax.shard_map(
        shards,
        mesh=mesh,
        in_specs=placed,
        out_specs=(P("wide", "field", None), P("wide", "field", None)),
        check_vma=False,
    )
```

profile of v0, /device:TPU:1, one launch (start us, length us, event | category | flops | bytes accessed | tf_op | source)
XLA Modules:
  0.0 289.1 jit_solution(15380336671605652760)
XLA Ops:
  3.8 10.3 %all-to-all-start.1 = ((bf16[64,16,512]{2,1,0:T(8,128)(2,1)}), bf16[64,16,512]{2,1,0:T(8,128)(2,1)S(1)}, u32[]{:S(2)}, u32[]{:S(2)}) async-start(bf16[64,16,512]{2,1,0:T(8,128)(2,1)} %broadcast_select_fusion), calls=%async_computation.1 | async-start | bytes 2097152 | tf_op jit(solution)/shard_map/all_to_all | solution.py:78
  14.1 36.5 %while.13 = (s32[]{:T(128)}, bf16[8,512,512]{2,1,0:T(8,128)(2,1)}, f32[8,3,1024]{2,0,1:T(8,128)}, f32[8,1024]{1,0:T(8,128)}, f32[8,3,1024]{2,0,1:T(8,128)}, /*index=5*/s32[]{:T(128)}, f32[]{:T(128)}) while((s32[]{:T(128)}, bf16[8,512,512]{2,1,0:T(8,128)(2,1)}, f32[8,3,1024]{2,0,1:T(8,128)}, f32[8,1024]{1,0:T(8,128)}, f32[8,3,1024]{2,0,1:T(8,128)}, ...), condition=%wide.region_4.5_spmd, body=%wide.region_3.4_spmd.sunk | while | flops 540100608 | bytes 7365209 | solution.py:73
  17.1 1.6 fusion.63
  21.7 1.5 fusion.63
  26.2 1.6 fusion.63
  30.8 1.6 fusion.63
  35.3 1.6 fusion.63
  39.9 1.6 fusion.63
  44.4 1.6 fusion.63
  49.0 1.5 fusion.63
  50.6 3.7 %convolution_convert_fusion.5 = bf16[8,128,512]{2,1,0:T(8,128)(2,1)S(1)} fusion(bf16[8,128,512]{2,1,0:T(8,128)(2,1)S(1)} %bitcast.90, bf16[8,512,512]{2,1,0:T(8,128)(2,1)} %get-tuple-element.143), kind=kOutput, calls=%fused_computation.83 | convolution fusion | flops 537395200 | bytes 6291456 | tf_op jit(solution)/shard_map/pfj,pij->pfi/dot_general | solution.py:79
  54.3 1.5 copy.71
  55.9 4.8 %all-to-all-start.2 = ((bf16[8,128,512]{2,0,1:T(8,128)(2,1)}), bf16[8,128,512]{2,0,1:T(8,128)(2,1)S(1)}, u32[]{:S(2)}, u32[]{:S(2)}) async-start(bf16[8,128,512]{2,0,1:T(8,128)(2,1)} %copy.71), calls=%async_computation.2 | async-start | bytes 2097152 | tf_op jit(solution)/shard_map/all_to_all | solution.py:82
  61.9 13.7 %all-to-all-done.2 = bf16[8,128,512]{2,0,1:T(8,128)(2,1)S(1)} async-done(((bf16[8,128,512]{2,0,1:T(8,128)(2,1)}), bf16[8,128,512]{2,0,1:T(8,128)(2,1)S(1)}, u32[]{:S(2)}, u32[]{:S(2)}) %all-to-all-start.2) | async-done | bytes 1048608 | tf_op jit(solution)/shard_map/all_to_all | solution.py:82
  75.7 11.8 %all-to-all-start = ((s32[64,2,1]{1,2,0:T(1,128)}), s32[64,2,1]{1,2,0:T(1,128)S(1)}, u32[]{:S(2)}, u32[]{:S(2)}) async-start(s32[64,2,1]{1,2,0:T(1,128)} %bitcast.11), calls=%async_computation | async-start | bytes 65536 | tf_op jit(solution)/shard_map/all_to_all | solution.py:98
  89.3 2.6 all_to_all.79
  91.9 6.4 %all-to-all-done = s32[64,2,1]{1,2,0:T(1,128)S(1)} async-done(((s32[64,2,1]{1,2,0:T(1,128)}), s32[64,2,1]{1,2,0:T(1,128)S(1)}, u32[]{:S(2)}, u32[]{:S(2)}) %all-to-all-start) | async-done | bytes 544 | tf_op jit(solution)/shard_map/all_to_all | solution.py:98
  98.3 5.8 %all-to-all-start.3 = ((bf16[64,2,8192]{2,1,0:T(2,128)(2,1)}), bf16[64,2,8192]{2,1,0:T(2,128)(2,1)S(1)}, u32[]{:S(2)}, u32[]{:S(2)}) async-start(bf16[64,2,8192]{2,1,0:T(2,128)(2,1)} %all_to_all.79), calls=%async_computation.3 | async-start | bytes 4194304 | tf_op jit(solution)/shard_map/all_to_all | solution.py:97
  104.3 48.8 %all-to-all-done.3 = bf16[64,2,8192]{2,1,0:T(2,128)(2,1)S(1)} async-done(((bf16[64,2,8192]{2,1,0:T(2,128)(2,1)}), bf16[64,2,8192]{2,1,0:T(2,128)(2,1)S(1)}, u32[]{:S(2)}, u32[]{:S(2)}) %all-to-all-start.3) | async-done | bytes 2097184 | tf_op jit(solution)/shard_map/all_to_all | solution.py:97
  153.1 2.2 all_to_all.81
  155.3 2.0 convolution_multiply_fusion.1
  157.3 3.5 %collective-permute-start = (f32[16,8192]{1,0:T(8,128)S(1)}, f32[16,8192]{1,0:T(8,128)S(1)}, u32[]{:S(2)}, u32[]{:S(2)}) collective-permute-start(f32[16,8192]{1,0:T(8,128)S(1)} %convolution_multiply_fusion.1), channel_id=1, source_target_pairs={{0,8},{8,16},{16,24},{24,32},{32,40},{40,48},{48,56},{56,64},{64,7... | collective-permute-start | bytes 1572872 | tf_op jit(solution)/shard_map/ppermute | solution.py:20
  160.9 1.3 collective-permute-start.1
  162.3 5.6 %collective-permute-done = f32[16,8192]{1,0:T(8,128)S(1)} collective-permute-done((f32[16,8192]{1,0:T(8,128)S(1)}, f32[16,8192]{1,0:T(8,128)S(1)}, u32[]{:S(2)}, u32[]{:S(2)}) %collective-permute-start) | collective-permute-done | bytes 524320 | tf_op jit(solution)/shard_map/ppermute | solution.py:20
  167.9 3.9 %collective-permute-done.1 = f32[16,8192]{1,0:T(8,128)S(1)} collective-permute-done((f32[16,8192]{1,0:T(8,128)S(1)}, f32[16,8192]{1,0:T(8,128)S(1)}, u32[]{:S(2)}, u32[]{:S(2)}) %collective-permute-start.1) | collective-permute-done | bytes 524320 | tf_op jit(solution)/shard_map/ppermute | solution.py:23
  173.4 2.6 all_to_all.82
  176.1 62.9 %all_to_all.99 = bf16[64,2,8192]{2,1,0:T(2,128)(2,1)} all-to-all(bf16[64,2,8192]{2,1,0:T(2,128)(2,1)} %all_to_all.82), channel_id=1, replica_groups=mesh['wide'=64,'field'=8] {'wide'}, dimensions={0} | all-to-all | bytes 4194304 | tf_op jit(solution)/shard_map/all_to_all | solution.py:121
  238.9 2.7 all_to_all.84
  242.5 22.5 %all_to_all.100 = bf16[64,16,512]{2,1,0:T(8,128)(2,1)S(1)} all-to-all(bf16[64,16,512]{2,1,0:T(8,128)(2,1)S(1)} %bitcast.86), channel_id=1, replica_groups=mesh['wide'=64,'field'=8] {'field'}, dimensions={0} | all-to-all | bytes 2097152 | tf_op jit(solution)/shard_map/all_to_all | solution.py:125
  265.8 1.6 copy.74
  267.4 4.5 %all-to-all-start.6 = ((bf16[8,128,512]{2,0,1:T(8,128)(2,1)}), bf16[8,128,512]{2,0,1:T(8,128)(2,1)S(1)}, u32[]{:S(2)}, u32[]{:S(2)}) async-start(bf16[8,128,512]{2,0,1:T(8,128)(2,1)} %copy.74), calls=%async_computation.6 | async-start | bytes 2097152 | tf_op jit(solution)/shard_map/all_to_all | solution.py:135
  272.7 14.2 %all-to-all-done.6 = bf16[8,128,512]{2,0,1:T(8,128)(2,1)S(1)} async-done(((bf16[8,128,512]{2,0,1:T(8,128)(2,1)}), bf16[8,128,512]{2,0,1:T(8,128)(2,1)S(1)}, u32[]{:S(2)}, u32[]{:S(2)}) %all-to-all-start.6) | async-done | bytes 1048608 | tf_op jit(solution)/shard_map/all_to_all | solution.py:135
  (264 shorter events, 35.3 us)
Async XLA Ops:
  0.6 1.4 copy-start
  3.8 46.8 %all-to-all-start.1 = ((bf16[64,16,512]{2,1,0:T(8,128)(2,1)}), bf16[64,16,512]{2,1,0:T(8,128)(2,1)S(1)}, u32[]{:S(2)}, u32[]{:S(2)}) async-start(bf16[64,16,512]{2,1,0:T(8,128)(2,1)} %broadcast_select_fusion), calls=%async_computation.1 | async-start | bytes 2097152 | tf_op jit(solution)/shard_map/all_to_all | solution.py:78
  54.3 6.4 %copy-start.2 = (s32[64,1]{0,1:T(1,128)S(1)}, s32[64,1]{0,1:T(1,128)}, u32[]{:S(2)}) copy-start(s32[64,1]{0,1:T(1,128)} %param.17) | copy-start | bytes 772
  54.3 6.7 %copy-start.7 = (s32[64]{0:T(128)S(1)}, s32[64]{0:T(128)}, u32[]{:S(2)}) copy-start(s32[64]{0:T(128)} %param.18) | copy-start | bytes 772
  55.9 19.8 %all-to-all-start.2 = ((bf16[8,128,512]{2,0,1:T(8,128)(2,1)}), bf16[8,128,512]{2,0,1:T(8,128)(2,1)S(1)}, u32[]{:S(2)}, u32[]{:S(2)}) async-start(bf16[8,128,512]{2,0,1:T(8,128)(2,1)} %copy.71), calls=%async_computation.2 | async-start | bytes 2097152 | tf_op jit(solution)/shard_map/all_to_all | solution.py:82
  75.7 22.6 %all-to-all-start = ((s32[64,2,1]{1,2,0:T(1,128)}), s32[64,2,1]{1,2,0:T(1,128)S(1)}, u32[]{:S(2)}, u32[]{:S(2)}) async-start(s32[64,2,1]{1,2,0:T(1,128)} %bitcast.11), calls=%async_computation | async-start | bytes 65536 | tf_op jit(solution)/shard_map/all_to_all | solution.py:98
  98.3 54.9 %all-to-all-start.3 = ((bf16[64,2,8192]{2,1,0:T(2,128)(2,1)}), bf16[64,2,8192]{2,1,0:T(2,128)(2,1)S(1)}, u32[]{:S(2)}, u32[]{:S(2)}) async-start(bf16[64,2,8192]{2,1,0:T(2,128)(2,1)} %all_to_all.79), calls=%async_computation.3 | async-start | bytes 4194304 | tf_op jit(solution)/shard_map/all_to_all | solution.py:97
  104.3 51.0 %copy-start.4 = (f32[16]{0:T(128)S(1)}, f32[16]{0:T(128)}, u32[]{:S(2)}) copy-start(f32[16]{0:T(128)} %param.20) | copy-start | bytes 196
  155.3 6.9 %copy-start.3 = (s32[16,6]{0,1:T(8,128)S(1)}, s32[16,6]{0,1:T(8,128)}, u32[]{:S(2)}) copy-start(s32[16,6]{0,1:T(8,128)} %param.19) | copy-start | bytes 1156
  157.3 10.6 %collective-permute-start = (f32[16,8192]{1,0:T(8,128)S(1)}, f32[16,8192]{1,0:T(8,128)S(1)}, u32[]{:S(2)}, u32[]{:S(2)}) collective-permute-start(f32[16,8192]{1,0:T(8,128)S(1)} %convolution_multiply_fusion.1), channel_id=1, source_target_pairs={{0,8},{8,16},{16,24},{24,32},{32,40},{40,48},{48,56},{56,64},{64,7... | collective-permute-start | bytes 1572872 | tf_op jit(solution)/shard_map/ppermute | solution.py:20
  160.9 10.9 %collective-permute-start.1 = (f32[16,8192]{1,0:T(8,128)S(1)}, f32[16,8192]{1,0:T(8,128)S(1)}, u32[]{:S(2)}, u32[]{:S(2)}) collective-permute-start(f32[16,8192]{1,0:T(8,128)S(1)} %convolution_multiply_fusion.1), channel_id=1, source_target_pairs={{8,0},{16,8},{24,16},{32,24},{40,32},{48,40},{56,48},{64,56},{72,6... | collective-permute-start | bytes 1572872 | tf_op jit(solution)/shard_map/ppermute | solution.py:23
  242.5 22.6 %copy-start.1 = (bf16[8,512,512]{2,1,0:T(8,128)(2,1)S(1)}, bf16[8,512,512]{2,1,0:T(8,128)(2,1)}, u32[]{:S(2)}) copy-start(bf16[8,512,512]{2,1,0:T(8,128)(2,1)} %get-tuple-element.143) | copy-start | bytes 12582916
  267.4 19.5 %all-to-all-start.6 = ((bf16[8,128,512]{2,0,1:T(8,128)(2,1)}), bf16[8,128,512]{2,0,1:T(8,128)(2,1)S(1)}, u32[]{:S(2)}, u32[]{:S(2)}) async-start(bf16[8,128,512]{2,0,1:T(8,128)(2,1)} %copy.74), calls=%async_computation.6 | async-start | bytes 2097152 | tf_op jit(solution)/shard_map/all_to_all | solution.py:135
  286.9 1.0 copy-start.5
  286.9 1.0 copy-start.6
where the time goes:
time: 291 us; the launch traced here: 289 us
  waiting for transfers between devices  92.6 us (32%)
  blocking collectives  85.3 us (29%)
  starting transfers between devices  42 us (14%)
  local copies, waits for them, and re-layouts  37.1 us (13%)
  matrix products  22 us (8%)
  other arithmetic  7.57 us (3%)
    all_to_all x1, blocking collectives, shards(): lax.all_to_all(reply, 'wide', split_axis=0, concat_axis=0, tiled=True)  62.9 us
    all_to_all x1, waiting for transfers between devices, shards(): lax.all_to_all(outgoing, 'wide', split_axis=0, concat_axis=0, tiled=True)  48.8 us
    all_to_all x1, blocking collectives, shards(): lax.all_to_all(per_pair.reshape(grp_pairs, block, basis_count), 'field',...  22.5 us
    all_to_all x1, waiting for transfers between devices, shards(): lax.all_to_all(terms, 'field', split_axis=1, concat_axis=0, tiled=True)  14.2 us
    dynamic_slice x16, local copies, waits for them, and re-layouts, shards(): lax.map(lambda item: build_tile(item[0], item[1], item[2]), (fine_points,...  13.8 us
    all_to_all x1, waiting for transfers between devices, shards(): lax.all_to_all(contrib, 'field', split_axis=1, concat_axis=0, tiled=True)  13.7 us
    dot_general x8, matrix products, build_tile(): lax.dot_general(left, right, (((1,), (1,)), ((), ())), preferred_element_...  12.4 us
    all_to_all x1, starting transfers between devices, shards(): lax.all_to_all(slot_ids, 'wide', split_axis=0, concat_axis=0, tiled=True)  11.8 us
  transfers between devices with their start and end apart: 7, of which 6 were waited for; matrix products, arithmetic and copies ran while one was open for 13% of the time, Pallas kernels for 0%

commit v1 on v0

v1 whole, which is shorter than its diff:
```python
import math

import jax
import jax.numpy as jnp
from jax import lax
from jax.experimental import pallas as pl
from jax.experimental.pallas import tpu as pltpu
from jax.sharding import PartitionSpec as P

NB = 8
DIFFUSE = 0.125
MESH = pl.DeviceIdType.MESH
BF = jnp.bfloat16
F32 = jnp.float32
VMEM = pltpu.VMEM
LIMIT = 60 << 20

NY = 8
NW = 64
NF = 8
OFFSETS = sorted(
    [(dz, dy) for dz in range(8) for dy in range(8) if (dz, dy) != (0, 0)],
    key=lambda t: ((t[1] - t[0]) % 8, t[0]),
)


def peer(wide, offset):
    z, y = wide // NY, wide % NY
    return ((z + offset[0]) % (NW // NY)) * NY + (y + offset[1]) % NY


def iota(shape, dim):
    return lax.broadcasted_iota(jnp.int32, shape, dim)


def swap_matrix(rows, minor_out, minor_in):
    r, c = iota((rows, rows), 0), iota((rows, rows), 1)
    return (c == (r % minor_out) * minor_in + r // minor_out).astype(BF)


def dot(a, b, dims=((1,), (0,))):
    return lax.dot_general(a, b, (dims, ((), ())), preferred_element_type=F32)


def legendre_rows(x):
    scale = [math.sqrt((2 * n + 1) / 2.0) for n in range(NB)]
    rows = [jnp.full_like(x, scale[0]), x * scale[1]]
    for n in range(1, NB - 1):
        up = (2 * n + 1) / (n + 1) * scale[n + 1] / scale[n]
        down = n / (n + 1) * scale[n + 1] / scale[n - 1]
        rows.append(up * (x * rows[n]) - down * rows[n - 1])
    return rows


def basis_block(points, at, weight, out_ref, i, lanes):
    def row(d):
        return jnp.broadcast_to(points[i, d : d + 1, lanes], (NB, 128))

    first, second, third = (legendre_rows(row(at + d)) for d in range(3))
    sub = iota((NB, 128), 0)
    minor = third[0]
    for n in range(1, NB):
        minor = jnp.where(sub == n, third[n], minor)
    if weight is not None:
        minor = minor * row(weight)
    pairs = [second[b] * minor for b in range(NB)]
    for a in range(NB):
        block = jnp.concatenate([first[a] * pairs[b] for b in range(NB)], axis=0)
        out_ref[a * 64 : (a + 1) * 64, lanes] = block.astype(BF)


def project_kernel(
    pair_fine_ref,
    fine_ref,
    fine_pts_ref,
    coarse_pts_ref,
    weights_ref,
    tiles_ref,
    mixed_ref,
    picked,
    points,
    rows,
    left,
    right,
    contrib,
    swapped,
    send_sem,
    recv_sem,
):
    wide, field = lax.axis_index("wide"), lax.axis_index("field")
    barrier = pltpu.get_barrier_semaphore()
    for k in range(1, NF):
        pl.semaphore_signal(
            barrier, inc=1, device_id=(wide, (field + k) % NF), device_id_type=MESH
        )

    def pick(p, carry):
        picked[p] = fine_ref[pair_fine_ref[p]]
        return carry

    lax.fori_loop(0, 64, pick, 0)
    pl.semaphore_wait(barrier, NF - 1)
    for k in range(1, NF):
        to = (field + k) % NF
        pltpu.make_async_remote_copy(
            picked.at[pl.ds(to * 8, 8)],
            rows.at[:, pl.ds(field * 16, 16), :],
            send_sem.at[0],
            recv_sem.at[0],
            device_id=(wide, to),
            device_id_type=MESH,
        ).start()
    pltpu.make_async_copy(
        picked.at[pl.ds(field * 8, 8)], rows.at[:, pl.ds(field * 16, 16), :], recv_sem.at[0]
    ).start()

    for i in range(8):
        for d in range(3):
            points[i, d : d + 1, :] = coarse_pts_ref[d, i : i + 1, :]
            points[i, 3 + d : 4 + d, :] = fine_pts_ref[d, i : i + 1, :]
        points[i, 6:7, :] = weights_ref[i : i + 1, :]

    def build(i, carry):
        def chunk(l, c):
            lanes = pl.ds(pl.multiple_of(l * 128, 128), 128)
            basis_block(points, 0, 6, left, i, lanes)
            basis_block(points, 3, None, right, i, lanes)
            return c

        lax.fori_loop(0, 8, chunk, 0)

        def multiply(m, c):
            at = pl.ds(pl.multiple_of(m * 256, 256), 256)
            tiles_ref[i, at, :] = dot(left[at, :], right[...], ((1,), (1,))).astype(BF)
            return c

        lax.fori_loop(0, 2, multiply, 0)
        return carry

    lax.fori_loop(0, 8, build, 0)
    pltpu.make_async_copy(rows, rows, recv_sem.at[0]).wait()

    def project(i, carry):
        contrib[i] = dot(rows[i], tiles_ref[i], ((1,), (1,))).astype(BF)
        return carry

    lax.fori_loop(0, 8, project, 0)
    swap = swap_matrix(128, 8, 16)
    for k in range(NF):
        to = (field + k) % NF
        block = contrib[:, pl.ds(pl.multiple_of(to * 16, 16), 16), :].reshape(128, 512)
        swapped[k] = dot(swap, block).reshape(16, 8, 512).astype(BF)
        if k:
            pltpu.make_async_remote_copy(
                swapped.at[k],
                mixed_ref.at[:, pl.ds(field * 8, 8), :],
                send_sem.at[1],
                recv_sem.at[1],
                device_id=(wide, to),
                device_id_type=MESH,
            ).start()
        else:
            pltpu.make_async_copy(
                swapped.at[k], mixed_ref.at[:, pl.ds(field * 8, 8), :], recv_sem.at[1]
            ).start()
    for step in range(2):
        sent = swapped.at[pl.ds(0, NF - 1)]
        pltpu.make_async_copy(sent, sent, send_sem.at[step]).wait()
    pltpu.make_async_copy(mixed_ref, mixed_ref, recv_sem.at[1]).wait()


def coarse_kernel(
    meta_ref,
    mixed_ref,
    coarse_ref,
    back_ref,
    metas,
    stage,
    arrived,
    hot,
    pick,
    faces,
    inverse,
    solved,
    smooth,
    reply,
    send_sem,
    recv_sem,
):
    wide, field = lax.axis_index("wide"), lax.axis_index("field")
    row, quarter = wide // 4, wide % 4
    slab = pl.ds(pl.multiple_of(quarter * 128, 128), 128)
    barrier = pltpu.get_barrier_semaphore()
    for offset in OFFSETS:
        pl.semaphore_signal(
            barrier, inc=1, device_id=(peer(wide, offset), field), device_id_type=MESH
        )
    pl.semaphore_wait(barrier, NW - 1)

    def source(to):
        lanes = pl.ds(pl.multiple_of((to % 4) * 128, 128), 128)
        return mixed_ref.at[to // 4, :, lanes]

    def exchange(index, src, dst):
        for offset in OFFSETS:
            to = peer(wide, offset)
            pltpu.make_async_remote_copy(
                src(to),
                dst,
                send_sem.at[index],
                recv_sem.at[index],
                device_id=(to, field),
                device_id_type=MESH,
            ).start()
        pltpu.make_async_copy(src(wide), dst, recv_sem.at[index]).start()

    def wait(ref, sem):
        pltpu.make_async_copy(ref, ref, sem).wait()

    exchange(0, lambda to: meta_ref, metas.at[wide])
    exchange(1, source, arrived.at[wide])
    wait(metas, recv_sem.at[0])
    stage[...] = jnp.zeros_like(stage)
    for s in range(NW):
        stage[0, s : s + 1, :] = metas[s, :, 0:128]
        stage[1, s : s + 1, :] = metas[s, :, 128:256]
    lane128 = iota((1, 128), 1)
    element = iota((1024, 128), 0).astype(F32)

    def build_hot(k, carry):
        low, high = stage[0, pl.ds(2 * k, 1), :], stage[0, pl.ds(2 * k + 1, 1), :]
        ids = jnp.where(lane128 < 64, low, high)
        at = pl.ds(pl.multiple_of(k * 128, 128), 128)
        hot[:, at] = (element == ids).astype(F32).astype(BF)
        return carry

    lax.fori_loop(0, NW // 2, build_hot, 0)
    turned = jnp.transpose(stage[0])
    stage[0] = turned
    turned = jnp.transpose(stage[1])
    stage[1] = turned
    lane = iota((64, 128), 1)
    lane_b = iota((128, 128), 1)
    number = iota((64, 1024), 1).astype(F32)
    number_b = iota((16, 1024), 1).astype(F32)

    def build_rest(s, carry):
        ids = jnp.sum(jnp.where(lane == s, stage[0, 0:64, :], 0.0), axis=1, keepdims=True)
        at = pl.ds(pl.multiple_of(s * 64, 64), 64)
        pick[at, :] = (number == ids).astype(F32).astype(BF)
        values = jnp.sum(jnp.where(lane_b == s, stage[1], 0.0), axis=1, keepdims=True)
        count = jnp.zeros((16, 1024), F32)
        for face in range(6):
            count += (number_b == values[face * 16 : (face + 1) * 16]).astype(F32)
        at = pl.ds(pl.multiple_of(s * 16, 16), 16)
        faces[at, :] = count.astype(BF)
        inverse[at, :] = jnp.broadcast_to(values[96:112], (16, 128))
        return carry

    lax.fori_loop(0, NW, build_rest, 0)
    wait(arrived, recv_sem.at[1])

    def load_rows(m, carry):
        at = pl.ds(pl.multiple_of(m * 256, 256), 256)
        total = dot(hot[at, :], arrived[...].reshape(4096, 128)) * inverse[at, :]
        high = total.astype(BF)
        solved[at, 0:128] = high
        solved[at, 128:256] = (total - high.astype(F32)).astype(BF)
        inverse[at, :] = total
        return carry

    lax.fori_loop(0, 4, load_rows, 0)

    def smooth_rows(m, carry):
        at = pl.ds(pl.multiple_of(m * 256, 256), 256)
        both = dot(faces[at, :], solved[...])
        own = inverse[at, :]
        beside = both[:, 0:128] + both[:, 128:256]
        smooth[at, :] = (own + DIFFUSE * (beside - 6.0 * own)).astype(BF)
        return carry

    lax.fori_loop(0, 4, smooth_rows, 0)

    def gather_rows(m, carry):
        at = pl.ds(pl.multiple_of(m * 512, 512), 512)
        reply[at, :] = dot(pick[at, :], smooth[...]).astype(BF)
        return carry

    lax.fori_loop(0, 8, gather_rows, 0)
    exchange(
        2,
        lambda to: reply.at[pl.ds(pl.multiple_of(to * 64, 64), 64)],
        back_ref.at[row, :, slab],
    )
    exchange(
        3,
        lambda to: smooth.at[pl.ds(pl.multiple_of(to * 16, 16), 16)],
        coarse_ref.at[row, :, slab],
    )
    wait(back_ref, recv_sem.at[2])
    wait(coarse_ref, recv_sem.at[3])
    wait(metas.at[pl.ds(0, NW - 1)], send_sem.at[0])
    for index in (1, 2):
        wait(arrived.at[pl.ds(0, NW - 1)], send_sem.at[index])
    wait(smooth.at[pl.ds(0, 16 * (NW - 1))], send_sem.at[3])


def return_kernel(
    tiles_hbm, back_ref, terms_ref, tiles, swapped, rows, result, send_sem, recv_sem, tile_sem
):
    wide, field = lax.axis_index("wide"), lax.axis_index("field")
    load = pltpu.make_async_copy(tiles_hbm, tiles, tile_sem)
    load.start()
    barrier = pltpu.get_barrier_semaphore()
    for k in range(1, NF):
        pl.semaphore_signal(
            barrier, inc=1, device_id=(wide, (field + k) % NF), device_id_type=MESH
        )
    swap = swap_matrix(128, 16, 8)
    pl.semaphore_wait(barrier, NF - 1)
    for k in range(1, NF + 1):
        to = (field + k) % NF
        block = back_ref[:, pl.ds(pl.multiple_of(to * 8, 8), 8), :].astype(F32)
        block = block.reshape(128, 512).astype(BF)
        swapped[k - 1] = dot(swap, block).astype(BF).reshape(8, 16, 512)
        if k < NF:
            pltpu.make_async_remote_copy(
                swapped.at[k - 1],
                rows.at[:, pl.ds(field * 16, 16), :],
                send_sem.at[0],
                recv_sem.at[0],
                device_id=(wide, to),
                device_id_type=MESH,
            ).start()
        else:
            pltpu.make_async_copy(
                swapped.at[k - 1], rows.at[:, pl.ds(field * 16, 16), :], recv_sem.at[0]
            ).start()
    load.wait()
    pltpu.make_async_copy(rows, rows, recv_sem.at[0]).wait()

    def term(i, carry):
        result[i] = dot(rows[i], tiles[i]).astype(BF)
        return carry

    lax.fori_loop(0, 8, term, 0)
    for k in range(1, NF + 1):
        to = (field + k) % NF
        src = result.at[:, pl.ds(pl.multiple_of(to * 16, 16), 16), :]
        dst = terms_ref.at[pl.ds(field * 8, 8)]
        if k < NF:
            pltpu.make_async_remote_copy(
                src, dst, send_sem.at[1], recv_sem.at[1], device_id=(wide, to), device_id_type=MESH
            ).start()
        else:
            pltpu.make_async_copy(src, dst, recv_sem.at[1]).start()
    for step in range(2):
        sent = swapped.at[pl.ds(0, NF - 1)]
        pltpu.make_async_copy(sent, sent, send_sem.at[step]).wait()
    pltpu.make_async_copy(terms_ref, terms_ref, recv_sem.at[1]).wait()


def finish_kernel(
    pair_fine_ref, inverse_ref, terms_ref, coarse_ref, coarse_out_ref, fine_out_ref, total
):
    swap = swap_matrix(256, 16, 16)
    block = coarse_ref[...].reshape(256, 512)
    coarse_out_ref[...] = dot(swap, block).astype(BF).reshape(16, 16, 512)
    total[...] = jnp.zeros_like(total)

    def add(p, carry):
        e = pair_fine_ref[p]
        total[e] += terms_ref[p].astype(F32)
        return carry

    lax.fori_loop(0, 64, add, 0)

    def store(e, carry):
        fine_out_ref[e] = (inverse_ref[e] * total[e]).astype(BF)
        return carry

    lax.fori_loop(0, 32, store, 0)


def vmem():
    return pl.BlockSpec(memory_space=pltpu.VMEM)


def smem():
    return pl.BlockSpec(memory_space=pltpu.SMEM)


def anywhere():
    return pl.BlockSpec(memory_space=pl.ANY)


def call(kernel, outs, in_specs, out_specs, scratch, number=None, cost=None):
    params = {"vmem_limit_bytes": LIMIT}
    if number is not None:
        params.update(collective_id=number, has_side_effects=True)
    return pl.pallas_call(
        kernel,
        out_shape=[jax.ShapeDtypeStruct(shape, BF) for shape in outs],
        in_specs=in_specs,
        out_specs=out_specs,
        scratch_shapes=scratch,
        compiler_params=pltpu.CompilerParams(**params),
    )


def shards(
    fine_field_in,
    fine_points,
    coarse_points,
    quad_weights,
    pair_fine,
    pair_owner,
    pair_coarse,
    coarse_faces,
    coarse_inv_mass,
    fine_inv_mass,
):
    dma = pltpu.SemaphoreType.DMA
    tiles, mixed = call(
        project_kernel,
        [(8, 512, 512), (16, 64, 512)],
        [smem(), vmem(), vmem(), vmem(), vmem()],
        [vmem(), vmem()],
        [
            VMEM((64, 16, 512), BF),
            VMEM((8, 8, 1024), F32),
            VMEM((8, 128, 512), BF),
            VMEM((512, 1024), BF),
            VMEM((512, 1024), BF),
            VMEM((8, 128, 512), BF),
            VMEM((8, 16, 8, 512), BF),
            dma((2,)),
            dma((2,)),
        ],
        0,
    )(
        pair_fine,
        fine_field_in,
        jnp.transpose(fine_points, (1, 0, 2)),
        jnp.transpose(coarse_points, (1, 0, 2)),
        quad_weights,
    )
    ids = (pair_owner[:, 0] * 16 + pair_coarse).astype(F32)
    meta = jnp.concatenate(
        [
            ids,
            ids,
            coarse_faces.T.reshape(-1).astype(F32),
            coarse_inv_mass,
            jnp.zeros((16,), F32),
        ]
    ).reshape(1, 256)
    coarse, back = call(
        coarse_kernel,
        [(16, 16, 512), (16, 64, 512)],
        [vmem(), vmem()],
        [vmem(), vmem()],
        [
            VMEM((NW, 1, 256), F32),
            VMEM((2, 128, 128), F32),
            VMEM((NW, 64, 128), BF),
            VMEM((1024, 4096), BF),
            VMEM((4096, 1024), BF),
            VMEM((1024, 1024), BF),
            VMEM((1024, 128), F32),
            VMEM((1024, 256), BF),
            VMEM((1024, 128), BF),
            VMEM((4096, 128), BF),
            dma((4,)),
            dma((4,)),
        ],
        1,
    )(meta, mixed)
    (terms,) = call(
        return_kernel,
        [(64, 16, 512)],
        [anywhere(), vmem()],
        [vmem()],
        [
            VMEM((8, 512, 512), BF),
            VMEM((8, 8, 16, 512), BF),
            VMEM((8, 128, 512), BF),
            VMEM((8, 128, 512), BF),
            dma((2,)),
            dma((2,)),
            dma,
        ],
        2,
    )(tiles, back)
    return call(
        finish_kernel,
        [(16, 16, 512), (32, 16, 512)],
        [smem(), smem(), vmem(), vmem()],
        [vmem(), vmem()],
        [VMEM((32, 16, 512), F32)],
    )(pair_fine, fine_inv_mass, terms, coarse)


def solution(mesh):
    placed = (
        P("wide", "field", None),
        P(("wide", "field"), None, None),
        P(("wide", "field"), None, None),
        P(("wide", "field"), None),
        P("wide"),
        P("wide", None),
        P("wide"),
        P("wide", None),
        P("wide"),
        P("wide"),
    )
    return jax.shard_map(
        shards,
        mesh=mesh,
        in_specs=placed,
        out_specs=(P("wide", "field", None), P("wide", "field", None)),
        check_vma=False,
    )
```

time: 291 us -> 164 us (0.56)
  Pallas kernels: 0 us -> 161 us
  waiting for transfers between devices: 92.6 us -> 0 us
  blocking collectives: 85.3 us -> 0 us
  starting transfers between devices: 42 us -> 0 us
  local copies, waits for them, and re-layouts: 37.1 us -> 1.38 us
  matrix products: 22 us -> 0 us
  other arithmetic: 7.57 us -> 1.37 us
    pallas_call x0 -> x4, Pallas kernels: none -> 161 us  [the longest x1 81.2 us: shards(): call(coarse_kernel, [(16, 16, 512), (16, 64, 512)], [vmem(), vmem()], [vm...]
    all_to_all x2 -> x0, blocking collectives: 85.3 us -> none  [the longest x1 62.9 us: shards(): lax.all_to_all(reply, 'wide', split_axis=0, concat_axis=0, tiled=True)]
    all_to_all x5 -> x0, waiting for transfers between devices: 83.2 us -> none  [the longest x1 48.8 us: shards(): lax.all_to_all(outgoing, 'wide', split_axis=0, concat_axis=0, tiled=True)]
    all_to_all x5 -> x0, starting transfers between devices: 37.2 us -> none  [the longest x1 11.8 us: shards(): lax.all_to_all(slot_ids, 'wide', split_axis=0, concat_axis=0, tiled=True)]
    dot_general x16 -> x0, matrix products: 22 us -> none  [the longest x8 12.4 us: build_tile(): lax.dot_general(left, right, (((1,), (1,)), ((), ())), preferred_element_...]
    dynamic_slice x16 -> x0, local copies, waits for them, and re-layouts: 13.8 us -> none  [shards(): lax.map(lambda item: build_tile(item[0], item[1], item[2]), (fine_points,...]
    all_to_all x9 -> x0, local copies, waits for them, and re-layouts: 11.8 us -> none  [the longest x2 5.38 us: shards(): lax.all_to_all(reply, 'wide', split_axis=0, concat_axis=0, tiled=True)]
    ppermute x2 -> x0, waiting for transfers between devices: 9.5 us -> none  [the longest x1 5.63 us: with_halo(): lax.ppermute(lax.slice_in_dim(block, block.shape[dim] - width, None, axis...]
  transfers between devices with their start and end apart: 7 -> 0, of which waited for: 6 -> 0; matrix products, arithmetic and copies ran while one was open for 13% -> 0% of each run, Pallas kernels for 0% -> 0%
where the time goes in v1:
time: 164 us
  Pallas kernels  161 us (98%)
    pallas_call x1, Pallas kernels, shards(): call(coarse_kernel, [(16, 16, 512), (16, 64, 512)], [vmem(), vmem()], [vm...  81.2 us
    pallas_call x1, Pallas kernels, shards(): call(project_kernel, [(8, 512, 512), (16, 64, 512)], [smem(), vmem(), vme...  43.1 us
    pallas_call x1, Pallas kernels, shards(): call(return_kernel, [(64, 16, 512)], [anywhere(), vmem()], [vmem()], [VME...  33.2 us

profile of v1, /device:TPU:1, one launch (start us, length us, event | category | flops | bytes accessed | tf_op | source)
XLA Modules:
  0.0 164.0 jit_solution(1235228219643296209)
XLA Ops:
  0.6 0.7 fusion
  1.3 0.7 convert_bitcast_fusion
  2.0 0.1 convert_element_type.15
  2.1 1.3 concatenate.3
  3.4 43.1 %shard_map.113 = (bf16[8,512,512]{2,1,0:T(8,128)(2,1)}, bf16[16,64,512]{2,1,0:T(8,128)(2,1)}) custom-call(s32[64]{0:T(128)} %pair_fine_ref.3, bf16[32,16,512]{2,1,0:T(8,128)(2,1)} %fine_ref.1, f32[3,8,1024]{2,1,0:T(8,128)} %bitcast.9, f32[3,8,1024]{2,1,0:T(8,128)} %bitcast.10, f32[8,1024]{1,0:T(8,128)} %weights_ref.1), custom_call_target="tpu_custom_call" | custom-call | tf_op jit(solution)/shard_map/pallas_call | solution.py:424
  46.5 81.2 %shard_map.114 = (bf16[16,16,512]{2,1,0:T(8,128)(2,1)}, bf16[16,64,512]{2,1,0:T(8,128)(2,1)}) custom-call(f32[1,256]{1,0:T(1,128)} %bitcast.11, bf16[16,64,512]{2,1,0:T(8,128)(2,1)} %get-tuple-element.7.mixed_ref), custom_call_target="tpu_custom_call" | custom-call | tf_op jit(solution)/shard_map/pallas_call | solution.py:458
  127.7 33.2 %shard_map.115.terms_ref = bf16[64,16,512]{2,1,0:T(8,128)(2,1)} custom-call(bf16[8,512,512]{2,1,0:T(8,128)(2,1)} %get-tuple-element.6.tiles_hbm, bf16[16,64,512]{2,1,0:T(8,128)(2,1)} %get-tuple-element.8.back_ref), custom_call_target="tpu_custom_call" | custom-call | tf_op jit(solution)/shard_map/pallas_call | solution.py:479
  160.9 3.1 %shard_map.116 = (bf16[16,16,512]{2,1,0:T(8,128)(2,1)}, bf16[32,16,512]{2,1,0:T(8,128)(2,1)}) custom-call(s32[64]{0:T(128)} %pair_fine_ref.3, f32[32]{0:T(128)} %inverse_ref.1, bf16[64,16,512]{2,1,0:T(8,128)(2,1)} %shard_map.115.terms_ref, bf16[16,16,512]{2,1,0:T(8,128)(2,1)} %get-tuple-element.9.coarse_ref), custom_call_target="tpu_custom_call" | custom-call | tf_op jit(solution)/shard_map/pallas_call | solution.py:495
  (1 shorter events, 0.0 us)

commit v2 on v0

v2 whole, which is shorter than its diff:
```python
import math

import jax
import jax.numpy as jnp
from jax import lax
from jax.experimental import pallas as pl
from jax.experimental.pallas import tpu as pltpu
from jax.sharding import PartitionSpec as P

NB = 8
DIFFUSE = 0.125
MESH = pl.DeviceIdType.MESH
BF = jnp.bfloat16
F32 = jnp.float32
VMEM = pltpu.VMEM
LIMIT = 60 << 20

NY = 8
NW = 64
NF = 8
NC = 4


def peer(wide, k):
    z, y = wide // NY, wide % NY
    a, b = k % NY, k // NY
    return ((z + a) % (NW // NY)) * NY + (y + a + b) % NY


def iota(shape, dim):
    return lax.broadcasted_iota(jnp.int32, shape, dim)


def swap_matrix(rows, minor_out, minor_in):
    r, c = iota((rows, rows), 0), iota((rows, rows), 1)
    return (c == (r % minor_out) * minor_in + r // minor_out).astype(BF)


def dot(a, b, dims=((1,), (0,))):
    return lax.dot_general(a, b, (dims, ((), ())), preferred_element_type=F32)


def legendre_rows(x):
    scale = [math.sqrt((2 * n + 1) / 2.0) for n in range(NB)]
    rows = [jnp.full_like(x, scale[0]), x * scale[1]]
    for n in range(1, NB - 1):
        up = (2 * n + 1) / (n + 1) * scale[n + 1] / scale[n]
        down = n / (n + 1) * scale[n + 1] / scale[n - 1]
        rows.append(up * (x * rows[n]) - down * rows[n - 1])
    return rows


def basis_block(points, at, weight, out_ref, i, lanes):
    def row(d):
        return jnp.broadcast_to(points[i, d : d + 1, lanes], (NB, 128))

    first, second, third = (legendre_rows(row(at + d)) for d in range(3))
    sub = iota((NB, 128), 0)
    minor = third[0]
    for n in range(1, NB):
        minor = jnp.where(sub == n, third[n], minor)
    if weight is not None:
        minor = minor * row(weight)
    pairs = [second[b] * minor for b in range(NB)]
    for a in range(NB):
        block = jnp.concatenate([first[a] * pairs[b] for b in range(NB)], axis=0)
        out_ref[a * 64 : (a + 1) * 64, lanes] = block.astype(BF)


def remap_kernel(
    pair_fine_ref,
    owner_ref,
    pair_coarse_ref,
    coarse_faces_ref,
    coarse_inverse_ref,
    fine_ref,
    fine_pts_ref,
    coarse_pts_ref,
    weights_ref,
    coarse_ref,
    terms_ref,
    picked,
    points,
    left,
    right,
    tiles,
    rows,
    contrib,
    blocks,
    mixed,
    meta,
    metas,
    stage,
    arrived,
    hot,
    pick,
    faces,
    inverse,
    load,
    solved,
    smooth,
    reply,
    back,
    spread,
    rows_back,
    result,
    send_sem,
    rows_sem,
    blocks_sem,
    arrived_sem,
    back_sem,
    rows_back_sem,
    other_sem,
):
    wide, field = lax.axis_index("wide"), lax.axis_index("field")
    barrier = pltpu.get_barrier_semaphore()

    def greet(k, carry):
        pl.semaphore_signal(
            barrier, inc=1, device_id=(peer(wide, k), field), device_id_type=MESH
        )
        return carry

    for k in range(1, NF):
        pl.semaphore_signal(
            barrier, inc=1, device_id=(wide, (field + k) % NF), device_id_type=MESH
        )
    lax.fori_loop(1, NW, greet, 0, unroll=3)

    def wait(ref, sem):
        pltpu.make_async_copy(ref, ref, sem).wait()

    def across(index, src, dst, sem):
        def one(k, carry):
            to = peer(wide, k)
            pltpu.make_async_remote_copy(
                src(to), dst, send_sem.at[index], sem, device_id=(to, field), device_id_type=MESH
            ).start()
            return carry

        lax.fori_loop(1, NW, one, 0, unroll=3)
        pltpu.make_async_copy(src(wide), dst, sem).start()

    def along(index, src, dst, sem):
        for k in range(1, NF):
            to = (field + k) % NF
            pltpu.make_async_remote_copy(
                src(to), dst, send_sem.at[index], sem, device_id=(wide, to), device_id_type=MESH
            ).start()
        pltpu.make_async_copy(src(field), dst, sem).start()

    def pick_rows(p, carry):
        picked[p] = fine_ref[pair_fine_ref[p]]
        return carry

    lax.fori_loop(0, 64, pick_rows, 0, unroll=4)

    lane = iota((1, 128), 1)
    for c in range(NC):
        ids = jnp.zeros((1, 128), F32)
        for r in range(16):
            p = (r % 8) * 8 + 2 * c + r // 8
            number = (owner_ref[p] * 16 + pair_coarse_ref[p]).astype(F32)
            ids = jnp.where(lane % 16 == r, number, ids)
        meta[:, c * 128 : (c + 1) * 128] = ids
    values = jnp.zeros((1, 128), F32)
    for e in range(16):
        for face in range(6):
            number = coarse_faces_ref[face, e].astype(F32)
            values = jnp.where(lane == face * 16 + e, number, values)
        values = jnp.where(lane == 96 + e, coarse_inverse_ref[e], values)
    meta[:, 512:640] = values

    for i in range(8):
        for d in range(3):
            points[i, d : d + 1, :] = coarse_pts_ref[d, i : i + 1, :]
            points[i, 3 + d : 4 + d, :] = fine_pts_ref[d, i : i + 1, :]
        points[i, 6:7, :] = weights_ref[i : i + 1, :]

    def build(i, carry):
        def chunk(l, c):
            lanes = pl.ds(pl.multiple_of(l * 128, 128), 128)
            basis_block(points, 0, 6, left, i, lanes)
            basis_block(points, 3, None, right, i, lanes)
            return c

        lax.fori_loop(0, 8, chunk, 0)
        tiles[i] = dot(left[...], right[...], ((1,), (1,))).astype(BF)
        return carry

    def project(i, carry):
        contrib[i] = dot(rows[i], tiles[i], ((1,), (1,))).astype(BF)
        return carry

    def term(i, carry):
        result[i] = dot(rows_back[i], tiles[i]).astype(BF)
        return carry

    swap = swap_matrix(256, 16, 16)

    def two(c):
        return pl.ds(2 * c, 2)

    def mine(width):
        return pl.ds(pl.multiple_of(field * width, width), width)

    def block_of(to):
        return pl.ds(pl.multiple_of(to * 16, 16), 16)

    def lanes_of(to):
        return pl.ds(pl.multiple_of((to % 4) * 128, 128), 128)

    def contribute(c):
        wait(rows.at[two(c)], rows_sem.at[c])
        lax.fori_loop(2 * c, 2 * c + 2, project, 0)
        along(
            1,
            lambda to: contrib.at[two(c), block_of(to), :],
            blocks.at[two(c), field],
            blocks_sem.at[c],
        )

    def transpose(c):
        wait(blocks.at[two(c)], blocks_sem.at[c])
        mixed[c] = dot(swap, blocks[two(c)].reshape(256, 512)).astype(BF).reshape(16, 16, 512)
        across(
            2,
            lambda to: mixed.at[c, to // 4, :, lanes_of(to)],
            arrived.at[c, wide],
            arrived_sem.at[c],
        )

    lax.fori_loop(0, 2, build, 0)
    pl.semaphore_wait(barrier, NW + NF - 2)
    for c in range(NC):
        along(
            0,
            lambda to: picked.at[pl.ds(to * 8 + 2 * c, 2)],
            rows.at[two(c), mine(16), :],
            rows_sem.at[c],
        )
    across(3, lambda to: meta, metas.at[wide], other_sem.at[0])
    lax.fori_loop(2, 4, build, 0)
    contribute(0)
    lax.fori_loop(4, 6, build, 0)
    contribute(1)
    transpose(0)
    lax.fori_loop(6, 8, build, 0)
    contribute(2)
    transpose(1)
    contribute(3)
    transpose(2)
    transpose(3)

    wait(metas, other_sem.at[0])
    stage[...] = jnp.zeros_like(stage)
    for s in range(NW):
        for c in range(NC + 1):
            stage[c, s : s + 1, :] = metas[s, :, c * 128 : (c + 1) * 128]
    element = iota((1024, 128), 0).astype(F32)
    own_lanes = iota((8, 128), 1) // 16 == iota((8, 128), 0)
    for c in range(NC):

        def build_hot(k, carry):
            eight = stage[c, pl.ds(pl.multiple_of(8 * k, 8), 8), :]
            ids = jnp.sum(jnp.where(own_lanes, eight, 0.0), axis=0, keepdims=True)
            at = pl.ds(pl.multiple_of(c * 1024 + k * 128, 128), 128)
            hot[:, at] = (element == ids).astype(F32).astype(BF)
            return carry

        lax.fori_loop(0, 8, build_hot, 0)
    for c in range(NC + 1):
        turned = jnp.transpose(stage[c])
        stage[c] = turned
    few = iota((16, 128), 1)
    many = iota((128, 128), 1)
    number = iota((16, 1024), 1).astype(F32)

    def build_rest(s, carry):
        at = pl.ds(pl.multiple_of(s * 16, 16), 16)
        for c in range(NC):
            ids = jnp.sum(jnp.where(few == s, stage[c, 0:16, :], 0.0), axis=1, keepdims=True)
            pick[c, at, :] = (number == ids).astype(F32).astype(BF)
        column = jnp.sum(jnp.where(many == s, stage[NC], 0.0), axis=1, keepdims=True)
        count = jnp.zeros((16, 1024), F32)
        for face in range(6):
            count += (number == column[face * 16 : (face + 1) * 16]).astype(F32)
        faces[at, :] = count.astype(BF)
        inverse[at, :] = jnp.broadcast_to(column[96:112], (16, 128))
        return carry

    lax.fori_loop(0, NW, build_rest, 0)

    for c in range(NC):
        wait(arrived.at[c], arrived_sem.at[c])

        def load_rows(m, carry):
            at = pl.ds(pl.multiple_of(m * 256, 256), 256)
            more = dot(hot[at, c * 1024 : (c + 1) * 1024], arrived[c].reshape(1024, 128))
            if c:
                more = load[at, :] + more
            if c < NC - 1:
                load[at, :] = more
            else:
                total = more * inverse[at, :]
                high = total.astype(BF)
                solved[at, 0:128] = high
                solved[at, 128:256] = (total - high.astype(F32)).astype(BF)
                load[at, :] = total
            return carry

        lax.fori_loop(0, 4, load_rows, 0)

    def smooth_rows(m, carry):
        at = pl.ds(pl.multiple_of(m * 256, 256), 256)
        both = dot(faces[at, :], solved[...])
        own = load[at, :]
        beside = both[:, 0:128] + both[:, 128:256]
        smooth[at, :] = (own + DIFFUSE * (beside - 6.0 * own)).astype(BF)
        return carry

    lax.fori_loop(0, 4, smooth_rows, 0)

    for c in range(NC):

        def gather_rows(m, carry):
            at = pl.ds(pl.multiple_of(m * 256, 256), 256)
            out = pl.ds(pl.multiple_of(m * 16, 16), 16)
            reply[c, out] = dot(pick[c, at, :], smooth[...]).astype(BF).reshape(16, 16, 128)
            return carry

        lax.fori_loop(0, 4, gather_rows, 0)
        across(
            4,
            lambda to: reply.at[c, to],
            back.at[c, wide // 4, :, lanes_of(wide)],
            back_sem.at[c],
        )
    across(
        5,
        lambda to: smooth.at[block_of(to)],
        coarse_ref.at[wide // 4, :, lanes_of(wide)],
        other_sem.at[1],
    )

    def finish(c):
        wait(rows_back.at[two(c)], rows_back_sem.at[c])
        lax.fori_loop(2 * c, 2 * c + 2, term, 0)
        along(
            7,
            lambda to: result.at[two(c), block_of(to), :],
            terms_ref.at[pl.ds(field * 8 + 2 * c, 2)],
            other_sem.at[2],
        )

    for c in range(NC):
        wait(back.at[c], back_sem.at[c])
        turned = dot(swap, back[c].reshape(256, 512)).astype(BF)
        spread[c] = turned.reshape(2, 8, 16, 512)
        along(
            6,
            lambda to: spread.at[c, :, to],
            rows_back.at[two(c), mine(16), :],
            rows_back_sem.at[c],
        )
        if c:
            finish(c - 1)
    finish(NC - 1)
    wait(coarse_ref, other_sem.at[1])
    wait(terms_ref, other_sem.at[2])
    for index in (0, 1, 6, 7):
        wait(picked.at[pl.ds(0, 56)], send_sem.at[index])
    wait(metas.at[pl.ds(0, NW - 1)], send_sem.at[3])
    for index in (2, 4):
        for c in range(NC):
            wait(arrived.at[c, pl.ds(0, NW - 1)], send_sem.at[index])
    wait(arrived.at[0, pl.ds(0, NW - 1)], send_sem.at[5])


def finish_kernel(
    pair_fine_ref, inverse_ref, terms_ref, coarse_ref, coarse_out_ref, fine_out_ref, total
):
    swap = swap_matrix(256, 16, 16)
    block = coarse_ref[...].reshape(256, 512)
    coarse_out_ref[...] = dot(swap, block).astype(BF).reshape(16, 16, 512)
    total[...] = jnp.zeros_like(total)

    def add(p, carry):
        e = pair_fine_ref[p]
        total[e] += terms_ref[p].astype(F32)
        return carry

    lax.fori_loop(0, 64, add, 0)

    def store(e, carry):
        fine_out_ref[e] = (inverse_ref[e] * total[e]).astype(BF)
        return carry

    lax.fori_loop(0, 32, store, 0)


def vmem():
    return pl.BlockSpec(memory_space=pltpu.VMEM)


def smem():
    return pl.BlockSpec(memory_space=pltpu.SMEM)


def call(kernel, outs, in_specs, out_specs, scratch, number=None, cost=None):
    params = {"vmem_limit_bytes": LIMIT}
    if number is not None:
        params.update(collective_id=number, has_side_effects=True)
    return pl.pallas_call(
        kernel,
        out_shape=[jax.ShapeDtypeStruct(shape, BF) for shape in outs],
        in_specs=in_specs,
        out_specs=out_specs,
        scratch_shapes=scratch,
        compiler_params=pltpu.CompilerParams(**params),
    )


def shards(
    fine_field_in,
    fine_points,
    coarse_points,
    quad_weights,
    pair_fine,
    pair_owner,
    pair_coarse,
    coarse_faces,
    coarse_inv_mass,
    fine_inv_mass,
):
    dma = pltpu.SemaphoreType.DMA
    coarse, terms = call(
        remap_kernel,
        [(16, 16, 512), (64, 16, 512)],
        [smem()] * 5 + [vmem()] * 4,
        [vmem(), vmem()],
        [
            VMEM((64, 16, 512), BF),
            VMEM((8, 8, 1024), F32),
            VMEM((512, 1024), BF),
            VMEM((512, 1024), BF),
            VMEM((8, 512, 512), BF),
            VMEM((8, 128, 512), BF),
            VMEM((8, 128, 512), BF),
            VMEM((8, 8, 16, 512), BF),
            VMEM((NC, 16, 16, 512), BF),
            VMEM((1, 640), F32),
            VMEM((NW, 1, 640), F32),
            VMEM((NC + 1, 128, 128), F32),
            VMEM((NC, NW, 16, 128), BF),
            VMEM((1024, 4096), BF),
            VMEM((NC, 1024, 1024), BF),
            VMEM((1024, 1024), BF),
            VMEM((1024, 128), F32),
            VMEM((1024, 128), F32),
            VMEM((1024, 256), BF),
            VMEM((1024, 128), BF),
            VMEM((NC, NW, 16, 128), BF),
            VMEM((NC, 16, 16, 512), BF),
            VMEM((NC, 2, 8, 16, 512), BF),
            VMEM((8, 128, 512), BF),
            VMEM((8, 128, 512), BF),
            dma((8,)),
            dma((NC,)),
            dma((NC,)),
            dma((NC,)),
            dma((NC,)),
            dma((NC,)),
            dma((3,)),
        ],
        0,
    )(
        pair_fine,
        pair_owner.reshape(64),
        pair_coarse,
        coarse_faces.T,
        coarse_inv_mass,
        fine_field_in,
        jnp.transpose(fine_points, (1, 0, 2)),
        jnp.transpose(coarse_points, (1, 0, 2)),
        quad_weights,
    )
    return call(
        finish_kernel,
        [(16, 16, 512), (32, 16, 512)],
        [smem(), smem(), vmem(), vmem()],
        [vmem(), vmem()],
        [VMEM((32, 16, 512), F32)],
    )(pair_fine, fine_inv_mass, terms, coarse)


def solution(mesh):
    placed = (
        P("wide", "field", None),
        P(("wide", "field"), None, None),
        P(("wide", "field"), None, None),
        P(("wide", "field"), None),
        P("wide"),
        P("wide", None),
        P("wide"),
        P("wide", None),
        P("wide"),
        P("wide"),
    )
    return jax.shard_map(
        shards,
        mesh=mesh,
        in_specs=placed,
        out_specs=(P("wide", "field", None), P("wide", "field", None)),
        check_vma=False,
    )
```

time: 291 us -> 115 us (0.40)
  Pallas kernels: 0 us -> 115 us
  waiting for transfers between devices: 92.6 us -> 0 us
  blocking collectives: 85.3 us -> 0 us
  starting transfers between devices: 42 us -> 0 us
  local copies, waits for them, and re-layouts: 37.1 us -> 0 us
  matrix products: 22 us -> 0 us
  other arithmetic: 7.57 us -> 0 us
    pallas_call x0 -> x2, Pallas kernels: none -> 115 us  [the longest x1 112 us: shards(): call(remap_kernel, [(16, 16, 512), (64, 16, 512)], [smem()] * 5 + [vmem()...]
    all_to_all x2 -> x0, blocking collectives: 85.3 us -> none  [the longest x1 62.9 us: shards(): lax.all_to_all(reply, 'wide', split_axis=0, concat_axis=0, tiled=True)]
    all_to_all x5 -> x0, waiting for transfers between devices: 83.2 us -> none  [the longest x1 48.8 us: shards(): lax.all_to_all(outgoing, 'wide', split_axis=0, concat_axis=0, tiled=True)]
    all_to_all x5 -> x0, starting transfers between devices: 37.2 us -> none  [the longest x1 11.8 us: shards(): lax.all_to_all(slot_ids, 'wide', split_axis=0, concat_axis=0, tiled=True)]
    dot_general x16 -> x0, matrix products: 22 us -> none  [the longest x8 12.4 us: build_tile(): lax.dot_general(left, right, (((1,), (1,)), ((), ())), preferred_element_...]
    dynamic_slice x16 -> x0, local copies, waits for them, and re-layouts: 13.8 us -> none  [shards(): lax.map(lambda item: build_tile(item[0], item[1], item[2]), (fine_points,...]
    all_to_all x9 -> x0, local copies, waits for them, and re-layouts: 11.8 us -> none  [the longest x2 5.38 us: shards(): lax.all_to_all(reply, 'wide', split_axis=0, concat_axis=0, tiled=True)]
    ppermute x2 -> x0, waiting for transfers between devices: 9.5 us -> none  [the longest x1 5.63 us: with_halo(): lax.ppermute(lax.slice_in_dim(block, block.shape[dim] - width, None, axis...]
  transfers between devices with their start and end apart: 7 -> 0, of which waited for: 6 -> 0; matrix products, arithmetic and copies ran while one was open for 13% -> 0% of each run, Pallas kernels for 0% -> 0%
where the time goes in v2:
time: 115 us
  Pallas kernels  115 us (100%)
    pallas_call x1, Pallas kernels, shards(): call(remap_kernel, [(16, 16, 512), (64, 16, 512)], [smem()] * 5 + [vmem()...  112 us
    pallas_call x1, Pallas kernels, shards(): call(finish_kernel, [(16, 16, 512), (32, 16, 512)], [smem(), smem(), vmem...  3.14 us

profile of v2, /device:TPU:1, one launch (start us, length us, event | category | flops | bytes accessed | tf_op | source)
XLA Modules:
  0.0 115.3 jit_solution(18005289078184377069)
XLA Ops:
  0.6 111.5 %shard_map.113 = (bf16[16,16,512]{2,1,0:T(8,128)(2,1)}, bf16[64,16,512]{2,1,0:T(8,128)(2,1)}) custom-call(s32[64]{0:T(128)} %pair_fine_ref.3, s32[64]{0:T(128)} %bitcast.7, s32[64]{0:T(128)} %pair_coarse_ref.1, s32[6,16]{1,0:T(8,128)} %bitcast.6, f32[16]{0:T(128)} %coarse_inverse_ref.1, bf16[32,16,512]{2,1,0:T(8,128)(2,1)} %fine_ref.1, ...), custom_call_target="tpu_custom_call" | custom-call | tf_op jit(solution)/shard_map/pallas_call | solution.py:437
  112.2 3.1 %shard_map.114 = (bf16[16,16,512]{2,1,0:T(8,128)(2,1)}, bf16[32,16,512]{2,1,0:T(8,128)(2,1)}) custom-call(s32[64]{0:T(128)} %pair_fine_ref.3, f32[32]{0:T(128)} %inverse_ref.1, bf16[64,16,512]{2,1,0:T(8,128)(2,1)} %get-tuple-element.4.terms_ref, bf16[16,16,512]{2,1,0:T(8,128)(2,1)} %get-tuple-element.5.coarse_ref), custom_call_target="tpu_custom_call" | custom-call | tf_op jit(solution)/shard_map/pallas_call | solution.py:488

commit v3 on v2

--- a/solution.py
+++ b/solution.py
@@ -22,9 +22,8 @@
 
 
 def peer(wide, k):
-    z, y = wide // NY, wide % NY
-    a, b = k % NY, k // NY
-    return ((z + a) % (NW // NY)) * NY + (y + a + b) % NY
+    z, y = lax.div(wide, NY), lax.rem(wide, NY)
+    return lax.rem(z + k % NY, NW // NY) * NY + lax.rem(y + k % NY + k // NY, NY)
 
 
 def iota(shape, dim):
@@ -73,12 +72,16 @@
     pair_coarse_ref,
     coarse_faces_ref,
     coarse_inverse_ref,
+    fine_hbm,
+    fine_pts_hbm,
+    coarse_pts_hbm,
+    weights_hbm,
+    coarse_ref,
+    terms_ref,
     fine_ref,
     fine_pts_ref,
     coarse_pts_ref,
     weights_ref,
-    coarse_ref,
-    terms_ref,
     picked,
     points,
     left,
@@ -111,49 +114,82 @@
     back_sem,
     rows_back_sem,
     other_sem,
+    input_sem,
 ):
     wide, field = lax.axis_index("wide"), lax.axis_index("field")
     barrier = pltpu.get_barrier_semaphore()
 
-    def greet(k, carry):
+    for k in range(1, NF):
+        pl.semaphore_signal(
+            barrier, inc=1, device_id=(wide, lax.rem(field + k, NF)), device_id_type=MESH
+        )
+    for k in range(1, NW):
         pl.semaphore_signal(
             barrier, inc=1, device_id=(peer(wide, k), field), device_id_type=MESH
         )
-        return carry
-
-    for k in range(1, NF):
-        pl.semaphore_signal(
-            barrier, inc=1, device_id=(wide, (field + k) % NF), device_id_type=MESH
-        )
-    lax.fori_loop(1, NW, greet, 0, unroll=3)
+    inputs = [
+        pltpu.make_async_copy(src, dst, input_sem.at[n])
+        for n, (src, dst) in enumerate(
+            (
+                (fine_hbm, fine_ref),
+                (coarse_pts_hbm, coarse_pts_ref),
+                (fine_pts_hbm, fine_pts_ref),
+                (weights_hbm, weights_ref),
+            )
+        )
+    ]
+    for copy in inputs:
+        copy.start()
 
     def wait(ref, sem):
         pltpu.make_async_copy(ref, ref, sem).wait()
 
     def across(index, src, dst, sem):
-        def one(k, carry):
+        for k in range(1, NW):
             to = peer(wide, k)
             pltpu.make_async_remote_copy(
                 src(to), dst, send_sem.at[index], sem, device_id=(to, field), device_id_type=MESH
             ).start()
-            return carry
-
-        lax.fori_loop(1, NW, one, 0, unroll=3)
         pltpu.make_async_copy(src(wide), dst, sem).start()
 
     def along(index, src, dst, sem):
         for k in range(1, NF):
-            to = (field + k) % NF
+            to = lax.rem(field + k, NF)
             pltpu.make_async_remote_copy(
                 src(to), dst, send_sem.at[index], sem, device_id=(wide, to), device_id_type=MESH
             ).start()
         pltpu.make_async_copy(src(field), dst, sem).start()
 
+    def two(c):
+        return pl.ds(2 * c, 2)
+
+    def mine(width):
+        return pl.ds(pl.multiple_of(field * width, width), width)
+
+    def block_of(to):
+        return pl.ds(pl.multiple_of(to * 16, 16), 16)
+
+    def lanes_of(to):
+        return pl.ds(pl.multiple_of(lax.rem(to, 4) * 128, 128), 128)
+
     def pick_rows(p, carry):
         picked[p] = fine_ref[pair_fine_ref[p]]
         return carry
 
-    lax.fori_loop(0, 64, pick_rows, 0, unroll=4)
+    inputs[0].wait()
+    lax.fori_loop(0, 64, pick_rows, 0, unroll=8)
+    pl.semaphore_wait(barrier, NW + NF - 2)
+
+    def send_rows(c):
+        along(
+            0,
+            lambda to: picked.at[pl.ds(to * 8 + 2 * c, 2)],
+            rows.at[two(c), mine(16), :],
+            rows_sem.at[c],
+        )
+
+    send_rows(0)
+    send_rows(1)
 
     lane = iota((1, 128), 1)
     for c in range(NC):
@@ -170,7 +206,10 @@
             values = jnp.where(lane == face * 16 + e, number, values)
         values = jnp.where(lane == 96 + e, coarse_inverse_ref[e], values)
     meta[:, 512:640] = values
-
+    across(3, lambda to: meta, metas.at[wide], other_sem.at[0])
+
+    for copy in inputs[1:]:
+        copy.wait()
     for i in range(8):
         for d in range(3):
             points[i, d : d + 1, :] = coarse_pts_ref[d, i : i + 1, :]
@@ -197,18 +236,6 @@
         return carry
 
     swap = swap_matrix(256, 16, 16)
-
-    def two(c):
-        return pl.ds(2 * c, 2)
-
-    def mine(width):
-        return pl.ds(pl.multiple_of(field * width, width), width)
-
-    def block_of(to):
-        return pl.ds(pl.multiple_of(to * 16, 16), 16)
-
-    def lanes_of(to):
-        return pl.ds(pl.multiple_of((to % 4) * 128, 128), 128)
 
     def contribute(c):
         wait(rows.at[two(c)], rows_sem.at[c])
@@ -225,29 +252,22 @@
         mixed[c] = dot(swap, blocks[two(c)].reshape(256, 512)).astype(BF).reshape(16, 16, 512)
         across(
             2,
-            lambda to: mixed.at[c, to // 4, :, lanes_of(to)],
+            lambda to: mixed.at[c, lax.div(to, 4), :, lanes_of(to)],
             arrived.at[c, wide],
             arrived_sem.at[c],
         )
 
     lax.fori_loop(0, 2, build, 0)
-    pl.semaphore_wait(barrier, NW + NF - 2)
-    for c in range(NC):
-        along(
-            0,
-            lambda to: picked.at[pl.ds(to * 8 + 2 * c, 2)],
-            rows.at[two(c), mine(16), :],
-            rows_sem.at[c],
-        )
-    across(3, lambda to: meta, metas.at[wide], other_sem.at[0])
+    contribute(0)
+    send_rows(2)
     lax.fori_loop(2, 4, build, 0)
-    contribute(0)
+    contribute(1)
+    send_rows(3)
+    transpose(0)
     lax.fori_loop(4, 6, build, 0)
-    contribute(1)
-    transpose(0)
-    lax.fori_loop(6, 8, build, 0)
     contribute(2)
     transpose(1)
+    lax.fori_loop(6, 8, build, 0)
     contribute(3)
     transpose(2)
     transpose(3)
@@ -294,52 +314,40 @@
     for c in range(NC):
         wait(arrived.at[c], arrived_sem.at[c])
 
-        def load_rows(m, carry):
-            at = pl.ds(pl.multiple_of(m * 256, 256), 256)
-            more = dot(hot[at, c * 1024 : (c + 1) * 1024], arrived[c].reshape(1024, 128))
-            if c:
-                more = load[at, :] + more
-            if c < NC - 1:
-                load[at, :] = more
-            else:
-                total = more * inverse[at, :]
-                high = total.astype(BF)
-                solved[at, 0:128] = high
-                solved[at, 128:256] = (total - high.astype(F32)).astype(BF)
-                load[at, :] = total
-            return carry
-
-        lax.fori_loop(0, 4, load_rows, 0)
+        more = dot(hot[:, c * 1024 : (c + 1) * 1024], arrived[c].reshape(1024, 128))
+        if c:
+            more = load[...] + more
+        if c < NC - 1:
+            load[...] = more
+        else:
+            total = more * inverse[...]
+            high = total.astype(BF)
+            solved[:, 0:128] = high
+            solved[:, 128:256] = (total - high.astype(F32)).astype(BF)
+            load[...] = total
 
     def smooth_rows(m, carry):
-        at = pl.ds(pl.multiple_of(m * 256, 256), 256)
+        at = pl.ds(pl.multiple_of(m * 512, 512), 512)
         both = dot(faces[at, :], solved[...])
         own = load[at, :]
         beside = both[:, 0:128] + both[:, 128:256]
         smooth[at, :] = (own + DIFFUSE * (beside - 6.0 * own)).astype(BF)
         return carry
 
-    lax.fori_loop(0, 4, smooth_rows, 0)
+    lax.fori_loop(0, 2, smooth_rows, 0)
 
     for c in range(NC):
-
-        def gather_rows(m, carry):
-            at = pl.ds(pl.multiple_of(m * 256, 256), 256)
-            out = pl.ds(pl.multiple_of(m * 16, 16), 16)
-            reply[c, out] = dot(pick[c, at, :], smooth[...]).astype(BF).reshape(16, 16, 128)
-            return carry
-
-        lax.fori_loop(0, 4, gather_rows, 0)
+        reply[c] = dot(pick[c], smooth[...]).astype(BF).reshape(NW, 16, 128)
         across(
             4,
             lambda to: reply.at[c, to],
-            back.at[c, wide // 4, :, lanes_of(wide)],
+            back.at[c, lax.div(wide, 4), :, lanes_of(wide)],
             back_sem.at[c],
         )
     across(
         5,
         lambda to: smooth.at[block_of(to)],
-        coarse_ref.at[wide // 4, :, lanes_of(wide)],
+        coarse_ref.at[lax.div(wide, 4), :, lanes_of(wide)],
         other_sem.at[1],
     )
 
@@ -405,6 +413,10 @@
 
 def smem():
     return pl.BlockSpec(memory_space=pltpu.SMEM)
+
+
+def anywhere():
+    return pl.BlockSpec(memory_space=pl.ANY)
 
 
 def call(kernel, outs, in_specs, out_specs, scratch, number=None, cost=None):
@@ -437,9 +449,13 @@
     coarse, terms = call(
         remap_kernel,
         [(16, 16, 512), (64, 16, 512)],
-        [smem()] * 5 + [vmem()] * 4,
+        [smem()] * 5 + [anywhere()] * 4,
         [vmem(), vmem()],
         [
+            VMEM((32, 16, 512), BF),
+            VMEM((3, 8, 1024), F32),
+            VMEM((3, 8, 1024), F32),
+            VMEM((8, 1024), F32),
             VMEM((64, 16, 512), BF),
             VMEM((8, 8, 1024), F32),
             VMEM((512, 1024), BF),
@@ -472,6 +488,7 @@
             dma((NC,)),
             dma((NC,)),
             dma((3,)),
+            dma((4,)),
         ],
         0,
     )(

time: 115 us -> 110 us (0.957)
  Pallas kernels: 115 us -> 109 us
    pallas_call x1, Pallas kernels: 112 us -> 106 us  [shards(): call(remap_kernel, [(16, 16, 512), (64, 16, 512)], [smem()] * 5 + [anywhe...]
where the time goes in v3:
time: 110 us
  Pallas kernels  109 us (99%)
    pallas_call x1, Pallas kernels, shards(): call(remap_kernel, [(16, 16, 512), (64, 16, 512)], [smem()] * 5 + [anywhe...  106 us
    pallas_call x1, Pallas kernels, shards(): call(finish_kernel, [(16, 16, 512), (32, 16, 512)], [smem(), smem(), vmem...  3.15 us

profile of v3, /device:TPU:1, one launch (start us, length us, event | category | flops | bytes accessed | tf_op | source)
XLA Modules:
  0.0 109.5 jit_solution(6585140351919755533)
XLA Ops:
  0.6 105.8 %shard_map.113 = (bf16[16,16,512]{2,1,0:T(8,128)(2,1)}, bf16[64,16,512]{2,1,0:T(8,128)(2,1)}) custom-call(s32[64]{0:T(128)} %pair_fine_ref.3, s32[64]{0:T(128)} %bitcast.7, s32[64]{0:T(128)} %pair_coarse_ref.1, s32[6,16]{1,0:T(8,128)} %bitcast.6, f32[16]{0:T(128)} %coarse_inverse_ref.1, bf16[32,16,512]{2,1,0:T(8,128)(2,1)} %fine_hbm.1, ...), custom_call_target="tpu_custom_call" | custom-call | tf_op jit(solution)/shard_map/pallas_call | solution.py:449
  106.4 3.1 %shard_map.114 = (bf16[16,16,512]{2,1,0:T(8,128)(2,1)}, bf16[32,16,512]{2,1,0:T(8,128)(2,1)}) custom-call(s32[64]{0:T(128)} %pair_fine_ref.3, f32[32]{0:T(128)} %inverse_ref.1, bf16[64,16,512]{2,1,0:T(8,128)(2,1)} %get-tuple-element.4.terms_ref, bf16[16,16,512]{2,1,0:T(8,128)(2,1)} %get-tuple-element.5.coarse_ref), custom_call_target="tpu_custom_call" | custom-call | tf_op jit(solution)/shard_map/pallas_call | solution.py:505

commit v4 on v3

--- a/solution.py
+++ b/solution.py
@@ -180,16 +180,16 @@
     lax.fori_loop(0, 64, pick_rows, 0, unroll=8)
     pl.semaphore_wait(barrier, NW + NF - 2)
 
-    def send_rows(c):
-        along(
-            0,
-            lambda to: picked.at[pl.ds(to * 8 + 2 * c, 2)],
-            rows.at[two(c), mine(16), :],
-            rows_sem.at[c],
-        )
-
-    send_rows(0)
-    send_rows(1)
+    def send_rows(*pairs):
+        for i in pairs:
+            along(
+                0,
+                lambda to: picked.at[to * 8 + i],
+                rows.at[i, mine(16), :],
+                rows_sem.at[i],
+            )
+
+    send_rows(0, 1, 2)
 
     lane = iota((1, 128), 1)
     for c in range(NC):
@@ -227,25 +227,18 @@
         tiles[i] = dot(left[...], right[...], ((1,), (1,))).astype(BF)
         return carry
 
-    def project(i, carry):
-        contrib[i] = dot(rows[i], tiles[i], ((1,), (1,))).astype(BF)
-        return carry
-
-    def term(i, carry):
-        result[i] = dot(rows_back[i], tiles[i]).astype(BF)
-        return carry
-
     swap = swap_matrix(256, 16, 16)
 
-    def contribute(c):
-        wait(rows.at[two(c)], rows_sem.at[c])
-        lax.fori_loop(2 * c, 2 * c + 2, project, 0)
-        along(
-            1,
-            lambda to: contrib.at[two(c), block_of(to), :],
-            blocks.at[two(c), field],
-            blocks_sem.at[c],
-        )
+    def contribute(*pairs):
+        for i in pairs:
+            wait(rows.at[i], rows_sem.at[i])
+            contrib[i] = dot(rows[i], tiles[i], ((1,), (1,))).astype(BF)
+            along(
+                1,
+                lambda to: contrib.at[i, block_of(to), :],
+                blocks.at[i, field],
+                blocks_sem.at[i // 2],
+            )
 
     def transpose(c):
         wait(blocks.at[two(c)], blocks_sem.at[c])
@@ -258,17 +251,17 @@
         )
 
     lax.fori_loop(0, 2, build, 0)
-    contribute(0)
-    send_rows(2)
+    contribute(0, 1)
+    send_rows(3, 4, 5)
     lax.fori_loop(2, 4, build, 0)
-    contribute(1)
-    send_rows(3)
+    contribute(2, 3)
+    send_rows(6, 7)
     transpose(0)
     lax.fori_loop(4, 6, build, 0)
-    contribute(2)
+    contribute(4, 5)
     transpose(1)
     lax.fori_loop(6, 8, build, 0)
-    contribute(3)
+    contribute(6, 7)
     transpose(2)
     transpose(3)
 
@@ -336,7 +329,7 @@
 
     lax.fori_loop(0, 2, smooth_rows, 0)
 
-    for c in range(NC):
+    def answer(c):
         reply[c] = dot(pick[c], smooth[...]).astype(BF).reshape(NW, 16, 128)
         across(
             4,
@@ -344,36 +337,43 @@
             back.at[c, lax.div(wide, 4), :, lanes_of(wide)],
             back_sem.at[c],
         )
-    across(
-        5,
-        lambda to: smooth.at[block_of(to)],
-        coarse_ref.at[lax.div(wide, 4), :, lanes_of(wide)],
-        other_sem.at[1],
-    )
-
-    def finish(c):
-        wait(rows_back.at[two(c)], rows_back_sem.at[c])
-        lax.fori_loop(2 * c, 2 * c + 2, term, 0)
-        along(
-            7,
-            lambda to: result.at[two(c), block_of(to), :],
-            terms_ref.at[pl.ds(field * 8 + 2 * c, 2)],
-            other_sem.at[2],
-        )
-
+
+    def finish(*pairs):
+        for i in pairs:
+            wait(rows_back.at[i], rows_back_sem.at[i])
+            result[i] = dot(rows_back[i], tiles[i]).astype(BF)
+            along(
+                7,
+                lambda to: result.at[i, block_of(to), :],
+                terms_ref.at[field * 8 + i],
+                other_sem.at[2],
+            )
+
+    answer(0)
+    answer(1)
     for c in range(NC):
         wait(back.at[c], back_sem.at[c])
         turned = dot(swap, back[c].reshape(256, 512)).astype(BF)
         spread[c] = turned.reshape(2, 8, 16, 512)
-        along(
-            6,
-            lambda to: spread.at[c, :, to],
-            rows_back.at[two(c), mine(16), :],
-            rows_back_sem.at[c],
-        )
+        for i in (2 * c, 2 * c + 1):
+            along(
+                6,
+                lambda to: spread.at[c, i % 2, to],
+                rows_back.at[i, mine(16), :],
+                rows_back_sem.at[i],
+            )
+        if c + 2 < NC:
+            answer(c + 2)
+        elif c + 2 == NC:
+            across(
+                5,
+                lambda to: smooth.at[block_of(to)],
+                coarse_ref.at[lax.div(wide, 4), :, lanes_of(wide)],
+                other_sem.at[1],
+            )
         if c:
-            finish(c - 1)
-    finish(NC - 1)
+            finish(2 * c - 2, 2 * c - 1)
+    finish(2 * NC - 2, 2 * NC - 1)
     wait(coarse_ref, other_sem.at[1])
     wait(terms_ref, other_sem.at[2])
     for index in (0, 1, 6, 7):
@@ -386,25 +386,27 @@
 
 
 def finish_kernel(
-    pair_fine_ref, inverse_ref, terms_ref, coarse_ref, coarse_out_ref, fine_out_ref, total
+    pair_fine_ref, inverse_ref, terms_ref, coarse_ref, coarse_out_ref, fine_out_ref, total, other
 ):
     swap = swap_matrix(256, 16, 16)
     block = coarse_ref[...].reshape(256, 512)
     coarse_out_ref[...] = dot(swap, block).astype(BF).reshape(16, 16, 512)
     total[...] = jnp.zeros_like(total)
+    other[...] = jnp.zeros_like(other)
 
     def add(p, carry):
-        e = pair_fine_ref[p]
-        total[e] += terms_ref[p].astype(F32)
+        first, second = pair_fine_ref[p], pair_fine_ref[p + 32]
+        total[first] += terms_ref[p].astype(F32)
+        other[second] += terms_ref[p + 32].astype(F32)
         return carry
 
-    lax.fori_loop(0, 64, add, 0)
+    lax.fori_loop(0, 32, add, 0, unroll=4)
 
     def store(e, carry):
-        fine_out_ref[e] = (inverse_ref[e] * total[e]).astype(BF)
+        fine_out_ref[e] = (inverse_ref[e] * (total[e] + other[e])).astype(BF)
         return carry
 
-    lax.fori_loop(0, 32, store, 0)
+    lax.fori_loop(0, 32, store, 0, unroll=4)
 
 
 def vmem():
@@ -482,11 +484,11 @@
             VMEM((8, 128, 512), BF),
             VMEM((8, 128, 512), BF),
             dma((8,)),
+            dma((8,)),
             dma((NC,)),
             dma((NC,)),
             dma((NC,)),
-            dma((NC,)),
-            dma((NC,)),
+            dma((8,)),
             dma((3,)),
             dma((4,)),
         ],
@@ -507,7 +509,7 @@
         [(16, 16, 512), (32, 16, 512)],
         [smem(), smem(), vmem(), vmem()],
         [vmem(), vmem()],
-        [VMEM((32, 16, 512), F32)],
+        [VMEM((32, 16, 512), F32), VMEM((32, 16, 512), F32)],
     )(pair_fine, fine_inv_mass, terms, coarse)
 
 

time: 110 us -> 109 us (level)
  Pallas kernels: 109 us -> 107 us
    pallas_call x1, Pallas kernels: 106 us -> 105 us  [shards(): call(remap_kernel, [(16, 16, 512), (64, 16, 512)], [smem()] * 5 + [anywhe...]
where the time goes in v4:
time: 109 us; the launch traced here: 108 us
  Pallas kernels  107 us (98%)
    pallas_call x1, Pallas kernels, shards(): call(remap_kernel, [(16, 16, 512), (64, 16, 512)], [smem()] * 5 + [anywhe...  105 us
    pallas_call x1, Pallas kernels, shards(): call(finish_kernel, [(16, 16, 512), (32, 16, 512)], [smem(), smem(), vmem...  2.79 us

profile of v4, /device:TPU:1, one launch (start us, length us, event | category | flops | bytes accessed | tf_op | source)
XLA Modules:
  0.0 108.0 jit_solution(17555956534204480090)
XLA Ops:
  0.6 104.5 %shard_map.113 = (bf16[16,16,512]{2,1,0:T(8,128)(2,1)}, bf16[64,16,512]{2,1,0:T(8,128)(2,1)}) custom-call(s32[64]{0:T(128)} %pair_fine_ref.3, s32[64]{0:T(128)} %bitcast.7, s32[64]{0:T(128)} %pair_coarse_ref.1, s32[6,16]{1,0:T(8,128)} %bitcast.6, f32[16]{0:T(128)} %coarse_inverse_ref.1, bf16[32,16,512]{2,1,0:T(8,128)(2,1)} %fine_hbm.1, ...), custom_call_target="tpu_custom_call" | custom-call | tf_op jit(solution)/shard_map/pallas_call | solution.py:451
  105.2 2.8 %shard_map.114 = (bf16[16,16,512]{2,1,0:T(8,128)(2,1)}, bf16[32,16,512]{2,1,0:T(8,128)(2,1)}) custom-call(s32[64]{0:T(128)} %pair_fine_ref.3, f32[32]{0:T(128)} %inverse_ref.1, bf16[64,16,512]{2,1,0:T(8,128)(2,1)} %get-tuple-element.4.terms_ref, bf16[16,16,512]{2,1,0:T(8,128)(2,1)} %get-tuple-element.5.coarse_ref), custom_call_target="tpu_custom_call" | custom-call | tf_op jit(solution)/shard_map/pallas_call | solution.py:507
